TPU v7x, 256 devices: a whole 4x4x8 slice. The times are simulated.
256 devices in a mesh: section: 128 (over z, y, x), attn: 2 (over core).
Axes of the slice: x: 4, y: 4, z: 8, core: 2. Of those that a mesh axis runs over, the one named last changes fastest.
Arguments:
- queries: bfloat16 [65536, 3072], P(('section', 'attn')), may hold values from -120 to 120
- keys: bfloat16 [65536, 1024], P(('section', 'attn')), may hold values from -2.5 to 2.5
- values: bfloat16 [65536, 1024], P(('section', 'attn')), may hold values from -4 to 4
- doc_ids: int32 [65536], replicated, may hold values from 0 to 127, never falling along the last dimension, each value on 1 to 1792 neighbouring positions
Outputs:
- attended: bfloat16 [65536, 3072], P(('section', 'attn'))
Inputs may be any that keep to these rules, and one draw needn't show every extreme that they name: `doc_ids`: along the pack the document numbers never fall, and a document holds at most 1792 tokens.
All inputs are finite; a program needn't handle non-finite values.
Results may differ from a plain program's by a relative error of at most 0.0028.
Values may be sent and summed in bfloat16 or wider, within the bound.
A program may use at most 64 MiB of HBM per device.

v0:
```python
import jax
import jax.numpy as jnp
from jax import lax
from jax.sharding import PartitionSpec as P

KV_HEADS = 8
HEAD_DIM = 128
GROUP = 3
REACH = 8


def passed_along(block, axis, distance):
    devices = range(lax.axis_size(axis))
    route = [(i - distance, i) for i in devices if i - distance in devices]
    return lax.ppermute(block, axis, route)


def fold_piece(carry, query_rows, key_rows, value_rows, query_pos, query_doc, key_pos, key_doc):
    row_max, total, weighted = carry
    head_size = query_rows.shape[-1]
    kv_count = query_rows.shape[1]
    key_heads = key_rows.reshape(key_rows.shape[0], kv_count, head_size)
    value_heads = value_rows.reshape(value_rows.shape[0], kv_count, head_size)
    scores = jnp.einsum(
        "qgrd,kgd->grqk", query_rows, key_heads, preferred_element_type=jnp.float32
    ) * head_size ** (-0.5)
    allowed = (key_pos[None, :] <= query_pos[:, None]) & (key_doc[None, :] == query_doc[:, None])
    scores = jnp.where(allowed, scores, -1e30)
    new_max = jnp.maximum(row_max, jnp.max(scores, axis=-1))
    rescale = jnp.exp(row_max - new_max)
    weights = jnp.exp(scores - new_max[..., None])
    total = total * rescale + jnp.sum(weights, axis=-1)
    product = jnp.einsum(
        "grqk,kgd->grqd",
        weights.astype(jnp.bfloat16),
        value_heads,
        preferred_element_type=jnp.float32,
    )
    weighted = weighted * rescale[..., None] + product
    return (new_max, total, weighted)


def fold_remote(carry, context, key_rows, value_rows, source):
    query_rows, doc_ids, owner = context
    rows = query_rows.shape[0]
    first = source * rows
    key_doc = lax.dynamic_slice_in_dim(doc_ids, jnp.maximum(first, 0), rows)
    query_doc = lax.dynamic_slice_in_dim(doc_ids, owner * rows, rows)
    needed = (source >= 0) & (source < owner) & (key_doc[rows - 1] == query_doc[0])
    key_pos = first + jnp.arange(rows, dtype=jnp.int32)
    query_pos = owner * rows + jnp.arange(rows, dtype=jnp.int32)

    def attend_piece(inner):
        return fold_piece(
            inner, query_rows, key_rows, value_rows, query_pos, query_doc, key_pos, key_doc
        )

    def skip_piece(inner):
        return inner

    return lax.cond(needed, attend_piece, skip_piece, carry)


def fold_window(carry, context, window_keys, window_values, first_source):
    rows = context[0].shape[0]
    pieces = window_keys.shape[0] // rows

    def one_piece(piece_num, inner):
        key_rows = lax.dynamic_slice_in_dim(window_keys, piece_num * rows, rows, 0)
        value_rows = lax.dynamic_slice_in_dim(window_values, piece_num * rows, rows, 0)
        return fold_remote(inner, context, key_rows, value_rows, first_source + piece_num)

    return lax.fori_loop(0, pieces, one_piece, carry)


def shards(queries, keys, values, doc_ids):
    rows = queries.shape[0]
    query_rows = queries.reshape(rows, KV_HEADS, GROUP, HEAD_DIM)
    cores = lax.axis_size("attn")
    chip = lax.axis_index("section")
    owner = chip * cores + lax.axis_index("attn")
    context = (query_rows, doc_ids, owner)
    query_doc = lax.dynamic_slice_in_dim(doc_ids, owner * rows, rows)
    query_pos = owner * rows + jnp.arange(rows, dtype=jnp.int32)
    stat_shape = (KV_HEADS, GROUP, rows)
    carry = (
        jnp.full(stat_shape, -1e30, jnp.float32),
        jnp.zeros(stat_shape, jnp.float32),
        jnp.zeros(stat_shape + (HEAD_DIM,), jnp.float32),
    )
    carry = fold_piece(carry, query_rows, keys, values, query_pos, query_doc, query_pos, query_doc)
    window = (
        lax.all_gather(keys, "attn", axis=0, tiled=True),
        lax.all_gather(values, "attn", axis=0, tiled=True),
    )
    carry = fold_window(carry, context, window[0], window[1], chip * cores)
    hops = (REACH + cores - 2) // cores
    for hop in range(1, hops + 1):
        window = passed_along((window[0], window[1]), "section", 1)
        carry = fold_window(carry, context, window[0], window[1], (chip - hop) * cores)
    row_max, total, weighted = carry
    result = (weighted / total[..., None]).astype(jnp.bfloat16)
    return result.transpose(2, 0, 1, 3).reshape(rows, -1)


def solution(mesh):
    placed = (
        P(("section", "attn"), None),
        P(("section", "attn"), None),
        P(("section", "attn"), None),
        P(),
    )
    return jax.shard_map(
        shards, mesh=mesh, in_specs=placed, out_specs=P(("section", "attn"), None), check_vma=False
    )
```

profile of v0, /device:TPU:46, one launch (start us, length us, event | category | flops | bytes accessed | tf_op | source)
XLA Modules:
  0.0 283.8 jit_solution(12785599930436756468)
XLA Ops:
  6.5 2.0 copy.34
  8.7 2.1 copy.35
  10.7 15.0 %all-gather.3.cloned.1.call-done = bf16[512,1024]{0,1:T(8,128)(2,1)} async-done(((bf16[256,1024]{0,1:T(8,128)(2,1)}), bf16[512,1024]{0,1:T(8,128)(2,1)}) %all-gather.3.cloned.1.call-update) | async-done | bytes 1048592 | tf_op jit(solution)/shard_map/all_gather | solution.py:93
  25.8 3.4 %collective-permute-start = (bf16[512,1024]{0,1:T(8,128)(2,1)}, bf16[512,1024]{0,1:T(8,128)(2,1)S(1)}, u32[]{:S(2)}, u32[]{:S(2)}) collective-permute-start(bf16[512,1024]{0,1:T(8,128)(2,1)} %all-gather.3.cloned.1.call-done), channel_id=1, source_target_pairs={{0,2},{2,4},{4,6},{6,8},{8,10},{10,12},{12,14},{14,16},{16,18},{18... | collective-permute-start | bytes 3145736 | tf_op jit(solution)/shard_map/ppermute | solution.py:15
  29.1 13.9 %all-gather.5.cloned.1.call-done = bf16[512,1024]{0,1:T(8,128)(2,1)} async-done(((bf16[256,1024]{0,1:T(8,128)(2,1)}), bf16[512,1024]{0,1:T(8,128)(2,1)}) %all-gather.5.cloned.1.call-update) | async-done | bytes 1048592 | tf_op jit(solution)/shard_map/all_gather | solution.py:94
  43.0 3.4 %collective-permute-start.1 = (bf16[512,1024]{0,1:T(8,128)(2,1)}, bf16[512,1024]{0,1:T(8,128)(2,1)S(1)}, u32[]{:S(2)}, u32[]{:S(2)}) collective-permute-start(bf16[512,1024]{0,1:T(8,128)(2,1)} %all-gather.5.cloned.1.call-done), channel_id=1, source_target_pairs={{0,2},{2,4},{4,6},{6,8},{8,10},{10,12},{12,14},{14,16},{16,18},{18... | collective-permute-start | bytes 3145736 | tf_op jit(solution)/shard_map/ppermute | solution.py:15
  46.4 7.5 %collective-permute-done = bf16[512,1024]{0,1:T(8,128)(2,1)S(1)} collective-permute-done((bf16[512,1024]{0,1:T(8,128)(2,1)}, bf16[512,1024]{0,1:T(8,128)(2,1)S(1)}, u32[]{:S(2)}, u32[]{:S(2)}) %collective-permute-start) | collective-permute-done | bytes 1048608 | tf_op jit(solution)/shard_map/ppermute | solution.py:15
  53.9 5.5 %collective-permute-start.2 = (bf16[512,1024]{0,1:T(8,128)(2,1)S(1)}, bf16[512,1024]{0,1:T(8,128)(2,1)S(1)}, u32[]{:S(2)}, u32[]{:S(2)}) collective-permute-start(bf16[512,1024]{0,1:T(8,128)(2,1)S(1)} %collective-permute-done), channel_id=1, source_target_pairs={{0,2},{2,4},{4,6},{6,8},{8,10},{10,12},{12,14},{14,16},{16,18},{18... | collective-permute-start | bytes 3145736 | tf_op jit(solution)/shard_map/ppermute | solution.py:15
  59.4 17.0 %collective-permute-done.1 = bf16[512,1024]{0,1:T(8,128)(2,1)S(1)} collective-permute-done((bf16[512,1024]{0,1:T(8,128)(2,1)}, bf16[512,1024]{0,1:T(8,128)(2,1)S(1)}, u32[]{:S(2)}, u32[]{:S(2)}) %collective-permute-start.1) | collective-permute-done | bytes 1048608 | tf_op jit(solution)/shard_map/ppermute | solution.py:15
  76.3 5.5 %collective-permute-start.3 = (bf16[512,1024]{0,1:T(8,128)(2,1)S(1)}, bf16[512,1024]{0,1:T(8,128)(2,1)}, u32[]{:S(2)}, u32[]{:S(2)}) collective-permute-start(bf16[512,1024]{0,1:T(8,128)(2,1)S(1)} %collective-permute-done.1), channel_id=1, source_target_pairs={{0,2},{2,4},{4,6},{6,8},{8,10},{10,12},{12,14},{14,16},{16,18},{18... | collective-permute-start | bytes 3145736 | tf_op jit(solution)/shard_map/ppermute | solution.py:15
  81.8 17.0 %collective-permute-done.2 = bf16[512,1024]{0,1:T(8,128)(2,1)S(1)} collective-permute-done((bf16[512,1024]{0,1:T(8,128)(2,1)S(1)}, bf16[512,1024]{0,1:T(8,128)(2,1)S(1)}, u32[]{:S(2)}, u32[]{:S(2)}) %collective-permute-start.2) | collective-permute-done | bytes 1048608 | tf_op jit(solution)/shard_map/ppermute | solution.py:15
  98.8 5.5 %collective-permute-start.4 = (bf16[512,1024]{0,1:T(8,128)(2,1)S(1)}, bf16[512,1024]{0,1:T(8,128)(2,1)}, u32[]{:S(2)}, u32[]{:S(2)}) collective-permute-start(bf16[512,1024]{0,1:T(8,128)(2,1)S(1)} %collective-permute-done.2), channel_id=1, source_target_pairs={{0,2},{2,4},{4,6},{6,8},{8,10},{10,12},{12,14},{14,16},{16,18},{18... | collective-permute-start | bytes 3145736 | tf_op jit(solution)/shard_map/ppermute | solution.py:15
  104.3 17.1 %collective-permute-done.3 = bf16[512,1024]{0,1:T(8,128)(2,1)} collective-permute-done((bf16[512,1024]{0,1:T(8,128)(2,1)S(1)}, bf16[512,1024]{0,1:T(8,128)(2,1)}, u32[]{:S(2)}, u32[]{:S(2)}) %collective-permute-start.3) | collective-permute-done | bytes 1048608 | tf_op jit(solution)/shard_map/ppermute | solution.py:15
  121.4 5.5 %collective-permute-start.5 = (bf16[512,1024]{0,1:T(8,128)(2,1)}, bf16[512,1024]{0,1:T(8,128)(2,1)}, u32[]{:S(2)}, u32[]{:S(2)}) collective-permute-start(bf16[512,1024]{0,1:T(8,128)(2,1)} %collective-permute-done.3), channel_id=1, source_target_pairs={{0,2},{2,4},{4,6},{6,8},{8,10},{10,12},{12,14},{14,16},{16,18},{18... | collective-permute-start | bytes 3145736 | tf_op jit(solution)/shard_map/ppermute | solution.py:15
  131.9 11.9 %collective-permute-done.4 = bf16[512,1024]{0,1:T(8,128)(2,1)} collective-permute-done((bf16[512,1024]{0,1:T(8,128)(2,1)S(1)}, bf16[512,1024]{0,1:T(8,128)(2,1)}, u32[]{:S(2)}, u32[]{:S(2)}) %collective-permute-start.4) | collective-permute-done | bytes 1048608 | tf_op jit(solution)/shard_map/ppermute | solution.py:15
  143.9 5.5 %collective-permute-start.6 = (bf16[512,1024]{0,1:T(8,128)(2,1)}, bf16[512,1024]{0,1:T(8,128)(2,1)}, u32[]{:S(2)}, u32[]{:S(2)}) collective-permute-start(bf16[512,1024]{0,1:T(8,128)(2,1)} %collective-permute-done.4), channel_id=1, source_target_pairs={{0,2},{2,4},{4,6},{6,8},{8,10},{10,12},{12,14},{14,16},{16,18},{18... | collective-permute-start | bytes 3145736 | tf_op jit(solution)/shard_map/ppermute | solution.py:15
  149.3 17.0 %collective-permute-done.5 = bf16[512,1024]{0,1:T(8,128)(2,1)} collective-permute-done((bf16[512,1024]{0,1:T(8,128)(2,1)}, bf16[512,1024]{0,1:T(8,128)(2,1)}, u32[]{:S(2)}, u32[]{:S(2)}) %collective-permute-start.5) | collective-permute-done | bytes 1048608 | tf_op jit(solution)/shard_map/ppermute | solution.py:15
  166.3 5.7 %collective-permute-start.7 = (bf16[512,1024]{0,1:T(8,128)(2,1)}, bf16[512,1024]{0,1:T(8,128)(2,1)}, u32[]{:S(2)}, u32[]{:S(2)}) collective-permute-start(bf16[512,1024]{0,1:T(8,128)(2,1)} %collective-permute-done.5), channel_id=1, source_target_pairs={{0,2},{2,4},{4,6},{6,8},{8,10},{10,12},{12,14},{14,16},{16,18},{18... | collective-permute-start | bytes 3145736 | tf_op jit(solution)/shard_map/ppermute | solution.py:15
  175.9 5.1 %fusion.74 = f32[8,3,256,128]{3,2,1,0:T(8,128)S(1)} fusion(f32[8,256,256,3]{2,1,3,0:T(8,128)} %copy-done, f32[8,3,256]{2,1,0:T(4,128)S(1)} %broadcast_maximum_fusion, pred[256,256]{0,1:T(8,128)(4,1)S(1)} %compare_and_fusion.5, f32[8,3,256]{2,1,0:T(4,128)S(1)} %get-tuple-element.2458, bf16[256,8,128,1]{2,1,0,3:T(8,128)(2,1)} %bitcast.175), kind=kOutput, calls=%fused_computation.111 | convolution fusion | flops 409731072 | bytes 10076160 | tf_op jit(solution)/shard_map/grqk,kgd->grqd/dot_general | solution.py:33
  181.1 7.0 %while.95 = (s32[]{:T(128)}, f32[8,3,256]{2,1,0:T(4,128)S(1)}, f32[8,3,256]{2,1,0:T(4,128)S(1)}, f32[8,3,256,128]{3,2,1,0:T(8,128)S(1)}, s32[]{:T(128)}, /*index...) while((s32[]{:T(128)}, f32[8,3,256]{2,1,0:T(4,128)S(1)}, ...), condition=%wide.region_7.8_spmd, body=%wide.region_2.7_spmd.sunk | while | flops 824390144 | bytes 30551492 | solution.py:73
  188.0 22.5 %while.96 = (s32[]{:T(128)}, f32[8,3,256]{2,1,0:T(4,128)S(1)}, f32[8,3,256]{2,1,0:T(4,128)S(1)}, f32[8,3,256,128]{3,2,1,0:T(8,128)S(1)}, s32[]{:T(128)}, /*index...) while((s32[]{:T(128)}, f32[8,3,256]{2,1,0:T(4,128)S(1)}, ...), condition=%wide.region_13.14_spmd, body=%wide.region_8.13_spmd.sunk | while | flops 824390144 | bytes 30551492 | solution.py:73
  191.2 8.1 %conditional.11 = ((f32[8,3,256]{2,1,0:T(4,128)S(1)}, f32[8,3,256]{2,1,0:T(4,128)S(1)}, f32[8,3,256,128]{3,2,1,0:T(8,128)S(1)})) conditional(s32[]{:T(128)} %convert_element_type.119, (f32[8,3,256]{2,1,0:T(4,128)S(1)}, f32[8,3,256]{2,1,0:T(4,128)S(1)}, f32[8,3,256,128]{3,2,1,0:T(8,128)S(1)}) %tuple.281, (s32[]{:T(128)}, s32[256]{0:T(256)S(1)}, ...), branch_computations={%region_9.9_spmd, %region_10.12_spmd} | conditional | flops 824390144 | bytes 30548058 | solution.py:61
  192.6 2.6 fusion.15
  196.7 2.6 multiply_add_fusion.2
  202.4 8.1 %conditional.11 = ((f32[8,3,256]{2,1,0:T(4,128)S(1)}, f32[8,3,256]{2,1,0:T(4,128)S(1)}, f32[8,3,256,128]{3,2,1,0:T(8,128)S(1)})) conditional(s32[]{:T(128)} %convert_element_type.119, (f32[8,3,256]{2,1,0:T(4,128)S(1)}, f32[8,3,256]{2,1,0:T(4,128)S(1)}, f32[8,3,256,128]{3,2,1,0:T(8,128)S(1)}) %tuple.281, (s32[]{:T(128)}, s32[256]{0:T(256)S(1)}, ...), branch_computations={%region_9.9_spmd, %region_10.12_spmd} | conditional | flops 824390144 | bytes 30548058 | solution.py:61
  203.8 2.6 fusion.15
  207.9 2.6 multiply_add_fusion.2
  210.5 22.6 %while.97 = (s32[]{:T(128)}, f32[8,3,256]{2,1,0:T(4,128)S(1)}, f32[8,3,256]{2,1,0:T(4,128)S(1)}, f32[8,3,256,128]{3,2,1,0:T(8,128)S(1)}, s32[]{:T(128)}, /*index...) while((s32[]{:T(128)}, f32[8,3,256]{2,1,0:T(4,128)S(1)}, ...), condition=%wide.region_19.20_spmd, body=%wide.region_14.19_spmd.sunk | while | flops 824390144 | bytes 30551492 | solution.py:73
  213.8 8.1 %conditional.12 = ((f32[8,3,256]{2,1,0:T(4,128)S(1)}, f32[8,3,256]{2,1,0:T(4,128)S(1)}, f32[8,3,256,128]{3,2,1,0:T(8,128)S(1)})) conditional(s32[]{:T(128)} %convert_element_type.120, (f32[8,3,256]{2,1,0:T(4,128)S(1)}, f32[8,3,256]{2,1,0:T(4,128)S(1)}, f32[8,3,256,128]{3,2,1,0:T(8,128)S(1)}) %tuple.284, (s32[]{:T(128)}, s32[256]{0:T(256)S(1)}, ...), branch_computations={%region_15.15_spmd, %region_16.18_spmd} | conditional | flops 824390144 | bytes 30548058 | solution.py:61
  215.3 2.6 fusion.28
  219.3 2.6 multiply_add_fusion.4
  225.0 8.1 %conditional.12 = ((f32[8,3,256]{2,1,0:T(4,128)S(1)}, f32[8,3,256]{2,1,0:T(4,128)S(1)}, f32[8,3,256,128]{3,2,1,0:T(8,128)S(1)})) conditional(s32[]{:T(128)} %convert_element_type.120, (f32[8,3,256]{2,1,0:T(4,128)S(1)}, f32[8,3,256]{2,1,0:T(4,128)S(1)}, f32[8,3,256,128]{3,2,1,0:T(8,128)S(1)}) %tuple.284, (s32[]{:T(128)}, s32[256]{0:T(256)S(1)}, ...), branch_computations={%region_15.15_spmd, %region_16.18_spmd} | conditional | flops 824390144 | bytes 30548058 | solution.py:61
  226.5 2.6 fusion.28
  230.5 2.6 multiply_add_fusion.4
  233.1 22.6 %while.98 = (s32[]{:T(128)}, f32[8,3,256]{2,1,0:T(4,128)S(1)}, f32[8,3,256]{2,1,0:T(4,128)S(1)}, f32[8,3,256,128]{3,2,1,0:T(8,128)S(1)}, s32[]{:T(128)}, /*index...) while((s32[]{:T(128)}, f32[8,3,256]{2,1,0:T(4,128)S(1)}, ...), condition=%wide.region_25.26_spmd, body=%wide.region_20.25_spmd.sunk | while | flops 824390144 | bytes 30551492 | solution.py:73
  236.3 8.1 %conditional.13 = ((f32[8,3,256]{2,1,0:T(4,128)S(1)}, f32[8,3,256]{2,1,0:T(4,128)S(1)}, f32[8,3,256,128]{3,2,1,0:T(8,128)S(1)})) conditional(s32[]{:T(128)} %convert_element_type.121, (f32[8,3,256]{2,1,0:T(4,128)S(1)}, f32[8,3,256]{2,1,0:T(4,128)S(1)}, f32[8,3,256,128]{3,2,1,0:T(8,128)S(1)}) %tuple.287, (s32[]{:T(128)}, s32[256]{0:T(256)S(1)}, ...), branch_computations={%region_21.21_spmd, %region_22.24_spmd} | conditional | flops 824390144 | bytes 30548058 | solution.py:61
  237.8 2.6 fusion.41
  241.9 2.6 multiply_add_fusion.6
  247.7 8.1 %conditional.13 = ((f32[8,3,256]{2,1,0:T(4,128)S(1)}, f32[8,3,256]{2,1,0:T(4,128)S(1)}, f32[8,3,256,128]{3,2,1,0:T(8,128)S(1)})) conditional(s32[]{:T(128)} %convert_element_type.121, (f32[8,3,256]{2,1,0:T(4,128)S(1)}, f32[8,3,256]{2,1,0:T(4,128)S(1)}, f32[8,3,256,128]{3,2,1,0:T(8,128)S(1)}) %tuple.287, (s32[]{:T(128)}, s32[256]{0:T(256)S(1)}, ...), branch_computations={%region_21.21_spmd, %region_22.24_spmd} | conditional | flops 824390144 | bytes 30548058 | solution.py:61
  249.1 2.6 fusion.41
  253.2 2.6 multiply_add_fusion.6
  255.8 14.8 %while.99 = (s32[]{:T(128)}, f32[8,3,256]{2,1,0:T(4,128)S(1)}, f32[8,3,256]{2,1,0:T(4,128)S(1)}, f32[8,3,256,128]{3,2,1,0:T(8,128)S(1)}, s32[]{:T(128)}, /*index...) while((s32[]{:T(128)}, f32[8,3,256]{2,1,0:T(4,128)S(1)}, ...), condition=%wide.region_31.32_spmd, body=%wide.region_26.31_spmd.sunk | while | flops 824390144 | bytes 30551492 | solution.py:73
  262.5 8.1 %conditional.14 = ((f32[8,3,256]{2,1,0:T(4,128)S(1)}, f32[8,3,256]{2,1,0:T(4,128)S(1)}, f32[8,3,256,128]{3,2,1,0:T(8,128)S(1)})) conditional(s32[]{:T(128)} %convert_element_type.122, (f32[8,3,256]{2,1,0:T(4,128)S(1)}, f32[8,3,256]{2,1,0:T(4,128)S(1)}, f32[8,3,256,128]{3,2,1,0:T(8,128)S(1)}) %tuple.290, (s32[]{:T(128)}, s32[256]{0:T(256)S(1)}, ...), branch_computations={%region_27.27_spmd, %region_28.30_spmd} | conditional | flops 824390144 | bytes 30548058 | solution.py:61
  264.0 2.6 fusion.54
  268.0 2.6 multiply_add_fusion.8
  270.6 2.3 copy.41
  272.9 2.3 divide_convert_fusion
  275.2 1.7 copy.42
  (119 shorter events, 48.1 us)
Async XLA Ops:
  6.5 19.2 %all-gather.3.cloned.1.call-start = ((), (), s32[]{:S(2)}) async-start(), calls=%async_computation | async-start | bytes 1572864 | tf_op jit(solution)/shard_map/all_gather | solution.py:93
  8.6 34.4 %all-gather.5.cloned.1.call-start = ((), (), s32[]{:S(2)}) async-start(), calls=%async_computation.1 | async-start | bytes 1572864 | tf_op jit(solution)/shard_map/all_gather | solution.py:94
  25.8 28.1 %collective-permute-start = (bf16[512,1024]{0,1:T(8,128)(2,1)}, bf16[512,1024]{0,1:T(8,128)(2,1)S(1)}, u32[]{:S(2)}, u32[]{:S(2)}) collective-permute-start(bf16[512,1024]{0,1:T(8,128)(2,1)} %all-gather.3.cloned.1.call-done), channel_id=1, source_target_pairs={{0,2},{2,4},{4,6},{6,8},{8,10},{10,12},{12,14},{14,16},{16,18},{18... | collective-permute-start | bytes 3145736 | tf_op jit(solution)/shard_map/ppermute | solution.py:15
  43.0 33.3 %collective-permute-start.1 = (bf16[512,1024]{0,1:T(8,128)(2,1)}, bf16[512,1024]{0,1:T(8,128)(2,1)S(1)}, u32[]{:S(2)}, u32[]{:S(2)}) collective-permute-start(bf16[512,1024]{0,1:T(8,128)(2,1)} %all-gather.5.cloned.1.call-done), channel_id=1, source_target_pairs={{0,2},{2,4},{4,6},{6,8},{8,10},{10,12},{12,14},{14,16},{16,18},{18... | collective-permute-start | bytes 3145736 | tf_op jit(solution)/shard_map/ppermute | solution.py:15
  53.9 73.0 %copy-start.2 = (bf16[512,1024]{0,1:T(8,128)(2,1)}, bf16[512,1024]{0,1:T(8,128)(2,1)S(1)}, u32[]{:S(2)}) copy-start(bf16[512,1024]{0,1:T(8,128)(2,1)S(1)} %collective-permute-done) | copy-start | bytes 3145732
  53.9 44.9 %collective-permute-start.2 = (bf16[512,1024]{0,1:T(8,128)(2,1)S(1)}, bf16[512,1024]{0,1:T(8,128)(2,1)S(1)}, u32[]{:S(2)}, u32[]{:S(2)}) collective-permute-start(bf16[512,1024]{0,1:T(8,128)(2,1)S(1)} %collective-permute-done), channel_id=1, source_target_pairs={{0,2},{2,4},{4,6},{6,8},{8,10},{10,12},{12,14},{14,16},{16,18},{18... | collective-permute-start | bytes 3145736 | tf_op jit(solution)/shard_map/ppermute | solution.py:15
  76.3 22.5 %copy-start.3 = (bf16[512,1024]{0,1:T(8,128)(2,1)}, bf16[512,1024]{0,1:T(8,128)(2,1)S(1)}, u32[]{:S(2)}) copy-start(bf16[512,1024]{0,1:T(8,128)(2,1)S(1)} %collective-permute-done.1) | copy-start | bytes 3145732
  76.3 45.0 %collective-permute-start.3 = (bf16[512,1024]{0,1:T(8,128)(2,1)S(1)}, bf16[512,1024]{0,1:T(8,128)(2,1)}, u32[]{:S(2)}, u32[]{:S(2)}) collective-permute-start(bf16[512,1024]{0,1:T(8,128)(2,1)S(1)} %collective-permute-done.1), channel_id=1, source_target_pairs={{0,2},{2,4},{4,6},{6,8},{8,10},{10,12},{12,14},{14,16},{16,18},{18... | collective-permute-start | bytes 3145736 | tf_op jit(solution)/shard_map/ppermute | solution.py:15
  98.8 33.0 %copy-start.1 = (bf16[512,1024]{0,1:T(8,128)(2,1)}, bf16[512,1024]{0,1:T(8,128)(2,1)S(1)}, u32[]{:S(2)}) copy-start(bf16[512,1024]{0,1:T(8,128)(2,1)S(1)} %collective-permute-done.2) | copy-start | bytes 3145732
  98.8 45.0 %collective-permute-start.4 = (bf16[512,1024]{0,1:T(8,128)(2,1)S(1)}, bf16[512,1024]{0,1:T(8,128)(2,1)}, u32[]{:S(2)}, u32[]{:S(2)}) collective-permute-start(bf16[512,1024]{0,1:T(8,128)(2,1)S(1)} %collective-permute-done.2), channel_id=1, source_target_pairs={{0,2},{2,4},{4,6},{6,8},{8,10},{10,12},{12,14},{14,16},{16,18},{18... | collective-permute-start | bytes 3145736 | tf_op jit(solution)/shard_map/ppermute | solution.py:15
  121.4 44.9 %collective-permute-start.5 = (bf16[512,1024]{0,1:T(8,128)(2,1)}, bf16[512,1024]{0,1:T(8,128)(2,1)}, u32[]{:S(2)}, u32[]{:S(2)}) collective-permute-start(bf16[512,1024]{0,1:T(8,128)(2,1)} %collective-permute-done.3), channel_id=1, source_target_pairs={{0,2},{2,4},{4,6},{6,8},{8,10},{10,12},{12,14},{14,16},{16,18},{18... | collective-permute-start | bytes 3145736 | tf_op jit(solution)/shard_map/ppermute | solution.py:15
  131.9 40.1 %copy-start = (f32[8,256,256,3]{2,1,3,0:T(8,128)}, f32[8,256,256,3]{2,1,3,0:T(8,128)S(1)}, u32[]{:S(2)}) copy-start(f32[8,256,256,3]{2,1,3,0:T(8,128)S(1)} %get-tuple-element.2461) | copy-start | bytes 18874372
  131.9 43.1 %copy-start.4 = (bf16[256,1024]{1,0:T(8,128)(2,1)S(1)}, bf16[256,1024]{1,0:T(8,128)(2,1)}, u32[]{:S(2)}) copy-start(bf16[256,1024]{1,0:T(8,128)(2,1)} %param.26) | copy-start | bytes 1572868
  143.9 111.9 %collective-permute-start.6 = (bf16[512,1024]{0,1:T(8,128)(2,1)}, bf16[512,1024]{0,1:T(8,128)(2,1)}, u32[]{:S(2)}, u32[]{:S(2)}) collective-permute-start(bf16[512,1024]{0,1:T(8,128)(2,1)} %collective-permute-done.4), channel_id=1, source_target_pairs={{0,2},{2,4},{4,6},{6,8},{8,10},{10,12},{12,14},{14,16},{16,18},{18... | collective-permute-start | bytes 3145736 | tf_op jit(solution)/shard_map/ppermute | solution.py:15
  166.3 89.4 %collective-permute-start.7 = (bf16[512,1024]{0,1:T(8,128)(2,1)}, bf16[512,1024]{0,1:T(8,128)(2,1)}, u32[]{:S(2)}, u32[]{:S(2)}) collective-permute-start(bf16[512,1024]{0,1:T(8,128)(2,1)} %collective-permute-done.5), channel_id=1, source_target_pairs={{0,2},{2,4},{4,6},{6,8},{8,10},{10,12},{12,14},{14,16},{16,18},{18... | collective-permute-start | bytes 3145736 | tf_op jit(solution)/shard_map/ppermute | solution.py:15
Sparse Core Ops, SparseCore 0:
  9.1 16.5 all-gather.2
  27.5 15.4 all-gather.4
where the time goes:
time: 285 us; the launch traced here: 284 us
  waiting for transfers between devices  116 us (41%)
  matrix products  42.7 us (15%)
  local copies, waits for them, and re-layouts  42.6 us (15%)
  starting transfers between devices  39.8 us (14%)
  other arithmetic  14.6 us (5%)
  loops' own time  14 us (5%)
  between operations  13.6 us (5%)
    ppermute x8, waiting for transfers between devices, passed_along(): return lax.ppermute(block, axis, route)  87.5 us
    ppermute x8, starting transfers between devices, passed_along(): return lax.ppermute(block, axis, route)  39.8 us
    dot_general x8, matrix products, fold_piece(): jnp.einsum('grqk,kgd->grqd', weights.astype(jnp.bfloat16), value_heads, p...  23 us
    dot_general x8, matrix products, fold_piece(): jnp.einsum('qgrd,kgd->grqk', query_rows, key_heads, preferred_element_typ...  19.7 us
    all_gather x1, waiting for transfers between devices, shards(): lax.all_gather(keys, 'attn', axis=0, tiled=True)  15 us
    all_gather x1, waiting for transfers between devices, shards(): lax.all_gather(values, 'attn', axis=0, tiled=True)  13.9 us
    another operation x5, loops' own time, fold_window(): return lax.fori_loop(0, pieces, one_piece, carry)  13.5 us
    reduce_sum x8, other arithmetic, fold_piece(): total = total * rescale + jnp.sum(weights, axis=-1)  10.9 us
  transfers between devices with their start and end apart: 10, of which 8 were waited for; matrix products, arithmetic and copies ran while one was open for 28% of the time, Pallas kernels for 0%

commit v1 on v0

--- a/solution.py
+++ b/solution.py
@@ -89,10 +89,13 @@
         jnp.zeros(stat_shape + (HEAD_DIM,), jnp.float32),
     )
     carry = fold_piece(carry, query_rows, keys, values, query_pos, query_doc, query_pos, query_doc)
-    window = (
-        lax.all_gather(keys, "attn", axis=0, tiled=True),
-        lax.all_gather(values, "attn", axis=0, tiled=True),
-    )
+
+    def words_store(original, bus_axis):
+        a_next = jnp.stack([original for _ in range(lax.axis_size(bus_axis))])
+        back = lax.all_to_all(a_next, bus_axis, 0, 0)
+        return jnp.concatenate(back, axis=0)
+
+    window = (words_store(keys, "attn"), lax.all_gather(values, "attn", axis=0, tiled=True))
     carry = fold_window(carry, context, window[0], window[1], chip * cores)
     hops = (REACH + cores - 2) // cores
     for hop in range(1, hops + 1):

time: 285 us -> 274 us (0.961)
  waiting for transfers between devices: 116 us -> 100 us
  blocking collectives: 0 us -> 4.58 us
    all_gather x1 -> x0, waiting for transfers between devices: 15 us -> none  [shards(): lax.all_gather(keys, 'attn', axis=0, tiled=True)]
    all_gather x1, waiting for transfers between devices: 13.9 us -> 7.25 us  [shards(): lax.all_gather(values, 'attn', axis=0, tiled=True)]
    ppermute x8, waiting for transfers between devices: 87.5 us -> 93 us  [passed_along(): return lax.ppermute(block, axis, route)]
    all_to_all x0 -> x1, blocking collectives: none -> 4.58 us  [words_store(): back = lax.all_to_all(a_next, bus_axis, 0, 0)]
    unnamed x15 -> x16, local copies, waits for them, and re-layouts: 7.86 us -> 5.63 us
  transfers between devices with their start and end apart: 10 -> 9, of which waited for: 8 -> 7; matrix products, arithmetic and copies ran while one was open for 28% -> 29% of each run, Pallas kernels for 0% -> 0%
where the time goes in v1:
time: 274 us; the launch traced here: 273 us
  waiting for transfers between devices  100 us (36%)
  matrix products  43.7 us (16%)
  local copies, waits for them, and re-layouts  40.9 us (15%)
  starting transfers between devices  39.9 us (15%)
  other arithmetic  15.9 us (6%)
  loops' own time  14 us (5%)
  between operations  13.6 us (5%)
  blocking collectives  4.58 us (2%)
    ppermute x8, waiting for transfers between devices, passed_along(): return lax.ppermute(block, axis, route)  93 us
    ppermute x8, starting transfers between devices, passed_along(): return lax.ppermute(block, axis, route)  39.9 us
    dot_general x8, matrix products, fold_piece(): jnp.einsum('grqk,kgd->grqd', weights.astype(jnp.bfloat16), value_heads, p...  23 us
    dot_general x8, matrix products, fold_piece(): jnp.einsum('qgrd,kgd->grqk', query_rows, key_heads, preferred_element_typ...  20.7 us
    another operation x5, loops' own time, fold_window(): return lax.fori_loop(0, pieces, one_piece, carry)  13.4 us
    reduce_sum x8, other arithmetic, fold_piece(): total = total * rescale + jnp.sum(weights, axis=-1)  10.9 us
    dynamic_slice x7, local copies, waits for them, and re-layouts, one_piece(): lax.dynamic_slice_in_dim(window_values, piece_num * rows, rows, 0)  8.92 us
    dynamic_slice x10, local copies, waits for them, and re-layouts, fold_remote(): key_doc = lax.dynamic_slice_in_dim(doc_ids, jnp.maximum(first, 0), rows)  7.78 us
  transfers between devices with their start and end apart: 9, of which 7 were waited for; matrix products, arithmetic and copies ran while one was open for 29% of the time, Pallas kernels for 0%

profile of v1, /device:TPU:46, one launch (start us, length us, event | category | flops | bytes accessed | tf_op | source)
XLA Modules:
  0.0 272.9 jit_solution(16235063923042756431)
XLA Ops:
  6.5 2.1 copy.35
  10.0 4.6 %all_to_all.5 = bf16[2,256,1024]{2,1,0:T(8,128)(2,1)S(1)} all-to-all(bf16[2,256,1024]{2,1,0:T(8,128)(2,1)S(1)} %pad_maximum_fusion), channel_id=1, replica_groups=mesh['section'=128,'attn'=2] {'attn'}, dimensions={0} | all-to-all | bytes 2097152 | tf_op jit(solution)/shard_map/all_to_all | solution.py:95
  15.1 3.4 %collective-permute-start = (bf16[512,1024]{0,1:T(8,128)(2,1)S(1)}, bf16[512,1024]{0,1:T(8,128)(2,1)}, u32[]{:S(2)}, u32[]{:S(2)}) collective-permute-start(bf16[512,1024]{0,1:T(8,128)(2,1)S(1)} %copy.86), channel_id=1, source_target_pairs={{0,2},{2,4},{4,6},{6,8},{8,10},{10,12},{12,14},{14,16},{16,18},{18... | collective-permute-start | bytes 3145736 | tf_op jit(solution)/shard_map/ppermute | solution.py:15
  18.5 7.3 %all-gather.2.cloned.1.call-done = bf16[512,1024]{0,1:T(8,128)(2,1)} async-done(((bf16[256,1024]{0,1:T(8,128)(2,1)}), bf16[512,1024]{0,1:T(8,128)(2,1)}) %all-gather.2.cloned.1.call-update) | async-done | bytes 1048592 | tf_op jit(solution)/shard_map/all_gather | solution.py:98
  25.8 3.4 %collective-permute-start.1 = (bf16[512,1024]{0,1:T(8,128)(2,1)}, bf16[512,1024]{0,1:T(8,128)(2,1)S(1)}, u32[]{:S(2)}, u32[]{:S(2)}) collective-permute-start(bf16[512,1024]{0,1:T(8,128)(2,1)} %all-gather.2.cloned.1.call-done), channel_id=1, source_target_pairs={{0,2},{2,4},{4,6},{6,8},{8,10},{10,12},{12,14},{14,16},{16,18},{18... | collective-permute-start | bytes 3145736 | tf_op jit(solution)/shard_map/ppermute | solution.py:15
  29.1 14.0 %collective-permute-done = bf16[512,1024]{0,1:T(8,128)(2,1)} collective-permute-done((bf16[512,1024]{0,1:T(8,128)(2,1)S(1)}, bf16[512,1024]{0,1:T(8,128)(2,1)}, u32[]{:S(2)}, u32[]{:S(2)}) %collective-permute-start) | collective-permute-done | bytes 1048608 | tf_op jit(solution)/shard_map/ppermute | solution.py:15
  43.1 5.5 %collective-permute-start.2 = (bf16[512,1024]{0,1:T(8,128)(2,1)}, bf16[512,1024]{0,1:T(8,128)(2,1)S(1)}, u32[]{:S(2)}, u32[]{:S(2)}) collective-permute-start(bf16[512,1024]{0,1:T(8,128)(2,1)} %collective-permute-done), channel_id=1, source_target_pairs={{0,2},{2,4},{4,6},{6,8},{8,10},{10,12},{12,14},{14,16},{16,18},{18... | collective-permute-start | bytes 3145736 | tf_op jit(solution)/shard_map/ppermute | solution.py:15
  48.6 16.9 %collective-permute-done.1 = bf16[512,1024]{0,1:T(8,128)(2,1)S(1)} collective-permute-done((bf16[512,1024]{0,1:T(8,128)(2,1)}, bf16[512,1024]{0,1:T(8,128)(2,1)S(1)}, u32[]{:S(2)}, u32[]{:S(2)}) %collective-permute-start.1) | collective-permute-done | bytes 1048608 | tf_op jit(solution)/shard_map/ppermute | solution.py:15
  65.5 5.5 %collective-permute-start.3 = (bf16[512,1024]{0,1:T(8,128)(2,1)S(1)}, bf16[512,1024]{0,1:T(8,128)(2,1)}, u32[]{:S(2)}, u32[]{:S(2)}) collective-permute-start(bf16[512,1024]{0,1:T(8,128)(2,1)S(1)} %collective-permute-done.1), channel_id=1, source_target_pairs={{0,2},{2,4},{4,6},{6,8},{8,10},{10,12},{12,14},{14,16},{16,18},{18... | collective-permute-start | bytes 3145736 | tf_op jit(solution)/shard_map/ppermute | solution.py:15
  71.0 17.0 %collective-permute-done.2 = bf16[512,1024]{0,1:T(8,128)(2,1)S(1)} collective-permute-done((bf16[512,1024]{0,1:T(8,128)(2,1)}, bf16[512,1024]{0,1:T(8,128)(2,1)S(1)}, u32[]{:S(2)}, u32[]{:S(2)}) %collective-permute-start.2) | collective-permute-done | bytes 1048608 | tf_op jit(solution)/shard_map/ppermute | solution.py:15
  88.0 5.5 %collective-permute-start.4 = (bf16[512,1024]{0,1:T(8,128)(2,1)S(1)}, bf16[512,1024]{0,1:T(8,128)(2,1)}, u32[]{:S(2)}, u32[]{:S(2)}) collective-permute-start(bf16[512,1024]{0,1:T(8,128)(2,1)S(1)} %collective-permute-done.2), channel_id=1, source_target_pairs={{0,2},{2,4},{4,6},{6,8},{8,10},{10,12},{12,14},{14,16},{16,18},{18... | collective-permute-start | bytes 3145736 | tf_op jit(solution)/shard_map/ppermute | solution.py:15
  93.5 17.1 %collective-permute-done.3 = bf16[512,1024]{0,1:T(8,128)(2,1)} collective-permute-done((bf16[512,1024]{0,1:T(8,128)(2,1)S(1)}, bf16[512,1024]{0,1:T(8,128)(2,1)}, u32[]{:S(2)}, u32[]{:S(2)}) %collective-permute-start.3) | collective-permute-done | bytes 1048608 | tf_op jit(solution)/shard_map/ppermute | solution.py:15
  110.5 5.5 %collective-permute-start.5 = (bf16[512,1024]{0,1:T(8,128)(2,1)}, bf16[512,1024]{0,1:T(8,128)(2,1)}, u32[]{:S(2)}, u32[]{:S(2)}) collective-permute-start(bf16[512,1024]{0,1:T(8,128)(2,1)} %collective-permute-done.3), channel_id=1, source_target_pairs={{0,2},{2,4},{4,6},{6,8},{8,10},{10,12},{12,14},{14,16},{16,18},{18... | collective-permute-start | bytes 3145736 | tf_op jit(solution)/shard_map/ppermute | solution.py:15
  119.6 2.2 fusion.67
  121.8 11.2 %collective-permute-done.4 = bf16[512,1024]{0,1:T(8,128)(2,1)} collective-permute-done((bf16[512,1024]{0,1:T(8,128)(2,1)S(1)}, bf16[512,1024]{0,1:T(8,128)(2,1)}, u32[]{:S(2)}, u32[]{:S(2)}) %collective-permute-start.4) | collective-permute-done | bytes 1048608 | tf_op jit(solution)/shard_map/ppermute | solution.py:15
  133.0 5.5 %collective-permute-start.6 = (bf16[512,1024]{0,1:T(8,128)(2,1)}, bf16[512,1024]{0,1:T(8,128)(2,1)}, u32[]{:S(2)}, u32[]{:S(2)}) collective-permute-start(bf16[512,1024]{0,1:T(8,128)(2,1)} %collective-permute-done.4), channel_id=1, source_target_pairs={{0,2},{2,4},{4,6},{6,8},{8,10},{10,12},{12,14},{14,16},{16,18},{18... | collective-permute-start | bytes 3145736 | tf_op jit(solution)/shard_map/ppermute | solution.py:15
  138.5 17.0 %collective-permute-done.5 = bf16[512,1024]{0,1:T(8,128)(2,1)} collective-permute-done((bf16[512,1024]{0,1:T(8,128)(2,1)}, bf16[512,1024]{0,1:T(8,128)(2,1)}, u32[]{:S(2)}, u32[]{:S(2)}) %collective-permute-start.5) | collective-permute-done | bytes 1048608 | tf_op jit(solution)/shard_map/ppermute | solution.py:15
  155.5 5.7 %collective-permute-start.7 = (bf16[512,1024]{0,1:T(8,128)(2,1)}, bf16[512,1024]{0,1:T(8,128)(2,1)}, u32[]{:S(2)}, u32[]{:S(2)}) collective-permute-start(bf16[512,1024]{0,1:T(8,128)(2,1)} %collective-permute-done.5), channel_id=1, source_target_pairs={{0,2},{2,4},{4,6},{6,8},{8,10},{10,12},{12,14},{14,16},{16,18},{18... | collective-permute-start | bytes 3145736 | tf_op jit(solution)/shard_map/ppermute | solution.py:15
  165.1 5.1 %fusion.74 = f32[8,3,256,128]{3,2,1,0:T(8,128)S(1)} fusion(f32[8,256,256,3]{2,1,3,0:T(8,128)} %copy-done, f32[8,3,256]{2,1,0:T(4,128)S(1)} %broadcast_maximum_fusion, pred[256,256]{0,1:T(8,128)(4,1)S(1)} %compare_and_fusion.5, f32[8,3,256]{2,1,0:T(4,128)S(1)} %get-tuple-element.2458, bf16[256,8,128,1]{2,1,0,3:T(8,128)(2,1)} %bitcast.179), kind=kOutput, calls=%fused_computation.111 | convolution fusion | flops 409731072 | bytes 10076160 | tf_op jit(solution)/shard_map/grqk,kgd->grqd/dot_general | solution.py:33
  170.2 6.4 %while.95 = (s32[]{:T(128)}, f32[8,3,256]{2,1,0:T(4,128)S(1)}, f32[8,3,256]{2,1,0:T(4,128)S(1)}, f32[8,3,256,128]{3,2,1,0:T(8,128)S(1)}, s32[]{:T(128)}, /*index...) while((s32[]{:T(128)}, f32[8,3,256]{2,1,0:T(4,128)S(1)}, ...), condition=%wide.region_7.8_spmd, body=%wide.region_2.7_spmd.sunk | while | flops 824390144 | bytes 30551492 | solution.py:73
  176.6 22.6 %while.96 = (s32[]{:T(128)}, f32[8,3,256]{2,1,0:T(4,128)S(1)}, f32[8,3,256]{2,1,0:T(4,128)S(1)}, f32[8,3,256,128]{3,2,1,0:T(8,128)S(1)}, s32[]{:T(128)}, /*index...) while((s32[]{:T(128)}, f32[8,3,256]{2,1,0:T(4,128)S(1)}, ...), condition=%wide.region_13.14_spmd, body=%wide.region_8.13_spmd.sunk | while | flops 824390144 | bytes 30551492 | solution.py:73
  179.8 8.1 %conditional.11 = ((f32[8,3,256]{2,1,0:T(4,128)S(1)}, f32[8,3,256]{2,1,0:T(4,128)S(1)}, f32[8,3,256,128]{3,2,1,0:T(8,128)S(1)})) conditional(s32[]{:T(128)} %convert_element_type.119, (f32[8,3,256]{2,1,0:T(4,128)S(1)}, f32[8,3,256]{2,1,0:T(4,128)S(1)}, f32[8,3,256,128]{3,2,1,0:T(8,128)S(1)}) %tuple.281, (s32[]{:T(128)}, s32[256]{0:T(256)S(1)}, ...), branch_computations={%region_9.9_spmd, %region_10.12_spmd} | conditional | flops 824390144 | bytes 30548058 | solution.py:61
  181.3 2.6 fusion.15
  185.3 2.6 multiply_add_fusion.2
  191.1 8.1 %conditional.11 = ((f32[8,3,256]{2,1,0:T(4,128)S(1)}, f32[8,3,256]{2,1,0:T(4,128)S(1)}, f32[8,3,256,128]{3,2,1,0:T(8,128)S(1)})) conditional(s32[]{:T(128)} %convert_element_type.119, (f32[8,3,256]{2,1,0:T(4,128)S(1)}, f32[8,3,256]{2,1,0:T(4,128)S(1)}, f32[8,3,256,128]{3,2,1,0:T(8,128)S(1)}) %tuple.281, (s32[]{:T(128)}, s32[256]{0:T(256)S(1)}, ...), branch_computations={%region_9.9_spmd, %region_10.12_spmd} | conditional | flops 824390144 | bytes 30548058 | solution.py:61
  192.6 2.6 fusion.15
  196.6 2.6 multiply_add_fusion.2
  199.2 22.6 %while.97 = (s32[]{:T(128)}, f32[8,3,256]{2,1,0:T(4,128)S(1)}, f32[8,3,256]{2,1,0:T(4,128)S(1)}, f32[8,3,256,128]{3,2,1,0:T(8,128)S(1)}, s32[]{:T(128)}, /*index...) while((s32[]{:T(128)}, f32[8,3,256]{2,1,0:T(4,128)S(1)}, ...), condition=%wide.region_19.20_spmd, body=%wide.region_14.19_spmd.sunk | while | flops 824390144 | bytes 30551492 | solution.py:73
  202.5 8.1 %conditional.12 = ((f32[8,3,256]{2,1,0:T(4,128)S(1)}, f32[8,3,256]{2,1,0:T(4,128)S(1)}, f32[8,3,256,128]{3,2,1,0:T(8,128)S(1)})) conditional(s32[]{:T(128)} %convert_element_type.120, (f32[8,3,256]{2,1,0:T(4,128)S(1)}, f32[8,3,256]{2,1,0:T(4,128)S(1)}, f32[8,3,256,128]{3,2,1,0:T(8,128)S(1)}) %tuple.284, (s32[]{:T(128)}, s32[256]{0:T(256)S(1)}, ...), branch_computations={%region_15.15_spmd, %region_16.18_spmd} | conditional | flops 824390144 | bytes 30548058 | solution.py:61
  204.0 2.6 fusion.28
  208.1 2.6 multiply_add_fusion.4
  213.7 8.1 %conditional.12 = ((f32[8,3,256]{2,1,0:T(4,128)S(1)}, f32[8,3,256]{2,1,0:T(4,128)S(1)}, f32[8,3,256,128]{3,2,1,0:T(8,128)S(1)})) conditional(s32[]{:T(128)} %convert_element_type.120, (f32[8,3,256]{2,1,0:T(4,128)S(1)}, f32[8,3,256]{2,1,0:T(4,128)S(1)}, f32[8,3,256,128]{3,2,1,0:T(8,128)S(1)}) %tuple.284, (s32[]{:T(128)}, s32[256]{0:T(256)S(1)}, ...), branch_computations={%region_15.15_spmd, %region_16.18_spmd} | conditional | flops 824390144 | bytes 30548058 | solution.py:61
  215.2 2.6 fusion.28
  219.3 2.6 multiply_add_fusion.4
  221.8 22.8 %while.98 = (s32[]{:T(128)}, f32[8,3,256]{2,1,0:T(4,128)S(1)}, f32[8,3,256]{2,1,0:T(4,128)S(1)}, f32[8,3,256,128]{3,2,1,0:T(8,128)S(1)}, s32[]{:T(128)}, /*index...) while((s32[]{:T(128)}, f32[8,3,256]{2,1,0:T(4,128)S(1)}, ...), condition=%wide.region_25.26_spmd, body=%wide.region_20.25_spmd.sunk | while | flops 824390144 | bytes 30551492 | solution.py:73
  225.2 8.1 %conditional.13 = ((f32[8,3,256]{2,1,0:T(4,128)S(1)}, f32[8,3,256]{2,1,0:T(4,128)S(1)}, f32[8,3,256,128]{3,2,1,0:T(8,128)S(1)})) conditional(s32[]{:T(128)} %convert_element_type.121, (f32[8,3,256]{2,1,0:T(4,128)S(1)}, f32[8,3,256]{2,1,0:T(4,128)S(1)}, f32[8,3,256,128]{3,2,1,0:T(8,128)S(1)}) %tuple.287, (s32[]{:T(128)}, s32[256]{0:T(256)S(1)}, ...), branch_computations={%region_21.21_spmd, %region_22.24_spmd} | conditional | flops 824390144 | bytes 30548058 | solution.py:61
  226.6 2.6 fusion.41
  230.7 2.6 multiply_add_fusion.6
  236.6 8.1 %conditional.13 = ((f32[8,3,256]{2,1,0:T(4,128)S(1)}, f32[8,3,256]{2,1,0:T(4,128)S(1)}, f32[8,3,256,128]{3,2,1,0:T(8,128)S(1)})) conditional(s32[]{:T(128)} %convert_element_type.121, (f32[8,3,256]{2,1,0:T(4,128)S(1)}, f32[8,3,256]{2,1,0:T(4,128)S(1)}, f32[8,3,256,128]{3,2,1,0:T(8,128)S(1)}) %tuple.287, (s32[]{:T(128)}, s32[256]{0:T(256)S(1)}, ...), branch_computations={%region_21.21_spmd, %region_22.24_spmd} | conditional | flops 824390144 | bytes 30548058 | solution.py:61
  238.0 2.6 fusion.41
  242.1 2.6 multiply_add_fusion.6
  244.7 15.0 %while.99 = (s32[]{:T(128)}, f32[8,3,256]{2,1,0:T(4,128)S(1)}, f32[8,3,256]{2,1,0:T(4,128)S(1)}, f32[8,3,256,128]{3,2,1,0:T(8,128)S(1)}, s32[]{:T(128)}, /*index...) while((s32[]{:T(128)}, f32[8,3,256]{2,1,0:T(4,128)S(1)}, ...), condition=%wide.region_31.32_spmd, body=%wide.region_26.31_spmd.sunk | while | flops 824390144 | bytes 30551492 | solution.py:73
  251.6 8.1 %conditional.14 = ((f32[8,3,256]{2,1,0:T(4,128)S(1)}, f32[8,3,256]{2,1,0:T(4,128)S(1)}, f32[8,3,256,128]{3,2,1,0:T(8,128)S(1)})) conditional(s32[]{:T(128)} %convert_element_type.122, (f32[8,3,256]{2,1,0:T(4,128)S(1)}, f32[8,3,256]{2,1,0:T(4,128)S(1)}, f32[8,3,256,128]{3,2,1,0:T(8,128)S(1)}) %tuple.290, (s32[]{:T(128)}, s32[256]{0:T(256)S(1)}, ...), branch_computations={%region_27.27_spmd, %region_28.30_spmd} | conditional | flops 824390144 | bytes 30548058 | solution.py:61
  253.1 2.6 fusion.54
  257.1 2.6 multiply_add_fusion.8
  259.7 2.3 copy.41
  262.1 2.3 divide_convert_fusion
  264.3 1.7 copy.42
  (120 shorter events, 48.4 us)
Async XLA Ops:
  6.5 111.2 %copy-start.4 = (bf16[256,1024]{1,0:T(8,128)(2,1)S(1)}, bf16[256,1024]{1,0:T(8,128)(2,1)}, u32[]{:S(2)}) copy-start(bf16[256,1024]{1,0:T(8,128)(2,1)} %param.25) | copy-start | bytes 1572868
  6.5 19.2 %all-gather.2.cloned.1.call-start = ((), (), s32[]{:S(2)}) async-start(), calls=%async_computation.1 | async-start | bytes 1572864 | tf_op jit(solution)/shard_map/all_gather | solution.py:98
  15.1 101.0 %copy-start.1 = (bf16[512,1024]{0,1:T(8,128)(2,1)}, bf16[512,1024]{0,1:T(8,128)(2,1)S(1)}, u32[]{:S(2)}) copy-start(bf16[512,1024]{0,1:T(8,128)(2,1)S(1)} %copy.86) | copy-start | bytes 3145732
  15.1 28.0 %collective-permute-start = (bf16[512,1024]{0,1:T(8,128)(2,1)S(1)}, bf16[512,1024]{0,1:T(8,128)(2,1)}, u32[]{:S(2)}, u32[]{:S(2)}) collective-permute-start(bf16[512,1024]{0,1:T(8,128)(2,1)S(1)} %copy.86), channel_id=1, source_target_pairs={{0,2},{2,4},{4,6},{6,8},{8,10},{10,12},{12,14},{14,16},{16,18},{18... | collective-permute-start | bytes 3145736 | tf_op jit(solution)/shard_map/ppermute | solution.py:15
  25.8 39.7 %collective-permute-start.1 = (bf16[512,1024]{0,1:T(8,128)(2,1)}, bf16[512,1024]{0,1:T(8,128)(2,1)S(1)}, u32[]{:S(2)}, u32[]{:S(2)}) collective-permute-start(bf16[512,1024]{0,1:T(8,128)(2,1)} %all-gather.2.cloned.1.call-done), channel_id=1, source_target_pairs={{0,2},{2,4},{4,6},{6,8},{8,10},{10,12},{12,14},{14,16},{16,18},{18... | collective-permute-start | bytes 3145736 | tf_op jit(solution)/shard_map/ppermute | solution.py:15
  43.1 44.8 %collective-permute-start.2 = (bf16[512,1024]{0,1:T(8,128)(2,1)}, bf16[512,1024]{0,1:T(8,128)(2,1)S(1)}, u32[]{:S(2)}, u32[]{:S(2)}) collective-permute-start(bf16[512,1024]{0,1:T(8,128)(2,1)} %collective-permute-done), channel_id=1, source_target_pairs={{0,2},{2,4},{4,6},{6,8},{8,10},{10,12},{12,14},{14,16},{16,18},{18... | collective-permute-start | bytes 3145736 | tf_op jit(solution)/shard_map/ppermute | solution.py:15
  65.5 22.5 %copy-start.3 = (bf16[512,1024]{0,1:T(8,128)(2,1)}, bf16[512,1024]{0,1:T(8,128)(2,1)S(1)}, u32[]{:S(2)}) copy-start(bf16[512,1024]{0,1:T(8,128)(2,1)S(1)} %collective-permute-done.1) | copy-start | bytes 3145732
  65.5 45.0 %collective-permute-start.3 = (bf16[512,1024]{0,1:T(8,128)(2,1)S(1)}, bf16[512,1024]{0,1:T(8,128)(2,1)}, u32[]{:S(2)}, u32[]{:S(2)}) collective-permute-start(bf16[512,1024]{0,1:T(8,128)(2,1)S(1)} %collective-permute-done.1), channel_id=1, source_target_pairs={{0,2},{2,4},{4,6},{6,8},{8,10},{10,12},{12,14},{14,16},{16,18},{18... | collective-permute-start | bytes 3145736 | tf_op jit(solution)/shard_map/ppermute | solution.py:15
  88.0 33.8 %copy-start.2 = (bf16[512,1024]{0,1:T(8,128)(2,1)}, bf16[512,1024]{0,1:T(8,128)(2,1)S(1)}, u32[]{:S(2)}) copy-start(bf16[512,1024]{0,1:T(8,128)(2,1)S(1)} %collective-permute-done.2) | copy-start | bytes 3145732
  88.0 45.0 %collective-permute-start.4 = (bf16[512,1024]{0,1:T(8,128)(2,1)S(1)}, bf16[512,1024]{0,1:T(8,128)(2,1)}, u32[]{:S(2)}, u32[]{:S(2)}) collective-permute-start(bf16[512,1024]{0,1:T(8,128)(2,1)S(1)} %collective-permute-done.2), channel_id=1, source_target_pairs={{0,2},{2,4},{4,6},{6,8},{8,10},{10,12},{12,14},{14,16},{16,18},{18... | collective-permute-start | bytes 3145736 | tf_op jit(solution)/shard_map/ppermute | solution.py:15
  110.5 44.9 %collective-permute-start.5 = (bf16[512,1024]{0,1:T(8,128)(2,1)}, bf16[512,1024]{0,1:T(8,128)(2,1)}, u32[]{:S(2)}, u32[]{:S(2)}) collective-permute-start(bf16[512,1024]{0,1:T(8,128)(2,1)} %collective-permute-done.3), channel_id=1, source_target_pairs={{0,2},{2,4},{4,6},{6,8},{8,10},{10,12},{12,14},{14,16},{16,18},{18... | collective-permute-start | bytes 3145736 | tf_op jit(solution)/shard_map/ppermute | solution.py:15
  121.8 39.4 %copy-start = (f32[8,256,256,3]{2,1,3,0:T(8,128)}, f32[8,256,256,3]{2,1,3,0:T(8,128)S(1)}, u32[]{:S(2)}) copy-start(f32[8,256,256,3]{2,1,3,0:T(8,128)S(1)} %get-tuple-element.2461) | copy-start | bytes 18874372
  121.8 42.3 %copy-start.5 = (bf16[256,1024]{1,0:T(8,128)(2,1)S(1)}, bf16[256,1024]{1,0:T(8,128)(2,1)}, u32[]{:S(2)}) copy-start(bf16[256,1024]{1,0:T(8,128)(2,1)} %param.26) | copy-start | bytes 1572868
  133.0 111.7 %collective-permute-start.6 = (bf16[512,1024]{0,1:T(8,128)(2,1)}, bf16[512,1024]{0,1:T(8,128)(2,1)}, u32[]{:S(2)}, u32[]{:S(2)}) collective-permute-start(bf16[512,1024]{0,1:T(8,128)(2,1)} %collective-permute-done.4), channel_id=1, source_target_pairs={{0,2},{2,4},{4,6},{6,8},{8,10},{10,12},{12,14},{14,16},{16,18},{18... | collective-permute-start | bytes 3145736 | tf_op jit(solution)/shard_map/ppermute | solution.py:15
  155.5 89.2 %collective-permute-start.7 = (bf16[512,1024]{0,1:T(8,128)(2,1)}, bf16[512,1024]{0,1:T(8,128)(2,1)}, u32[]{:S(2)}, u32[]{:S(2)}) collective-permute-start(bf16[512,1024]{0,1:T(8,128)(2,1)} %collective-permute-done.5), channel_id=1, source_target_pairs={{0,2},{2,4},{4,6},{6,8},{8,10},{10,12},{12,14},{14,16},{16,18},{18... | collective-permute-start | bytes 3145736 | tf_op jit(solution)/shard_map/ppermute | solution.py:15
Sparse Core Ops, SparseCore 0:
  9.1 16.5 all-gather.1
